TPU v7x, 128 devices: a whole 4x4x4 slice. The times are simulated.
128 devices in a mesh: energy: 4 (over z), cols: 32 (over x, y, core).
Axes of the slice: x: 4, y: 4, z: 4, core: 2. Of those that a mesh axis runs over, the one named last changes fastest.
Arguments:
- left_inverse: bfloat16 [12, 2, 1536, 1536], P('energy', None, 'cols'), parts along dimension 0, as said below
- regions: int32 [3, 1536], replicated, may hold values from 0 to 2
- region_mass: float32 [3], replicated, may hold values from 1 to 2.5
- region_alpha: float32 [3], replicated, may hold values from 0.1 to 0.5
- energy_grid: float32 [16], replicated, may hold values from 0.2 to 1
- energy_index: int32 [4], P('energy'), parts along dimension 0, may hold values from 0 to 15
Outputs:
- green: float32 [8, 2, 1536, 1536], P('energy', None, 'cols'), parts along dimension 0
There are 4 independent parts, one for each index of `energy`. A program takes and returns all parts, laid end to end along the dimension named above; an argument that names none is the same for every part. Nothing has to cross between parts.
Inputs may be any that keep to these rules, and one draw needn't show every extreme that they name: Every block of left_inverse is complex symmetric: both planes equal their transposes.
All inputs are finite; a program needn't handle non-finite values.
Results may differ from a plain program's by a relative error of at most 0.0024.
Values may be sent and summed in bfloat16 or wider, within the bound.
A program may use at most 128 MiB of HBM per device.

v0:
```python
import jax
import jax.numpy as jnp
from jax import lax
from jax.sharding import PartitionSpec as P


def complex_product(left, right):
    real = jnp.dot(left[0], right[0], preferred_element_type=jnp.float32) - jnp.dot(
        left[1], right[1], preferred_element_type=jnp.float32
    )
    imag = jnp.dot(left[0], right[1], preferred_element_type=jnp.float32) + jnp.dot(
        left[1], right[0], preferred_element_type=jnp.float32
    )
    return jnp.stack([real, imag])


def couplings(regions, region_mass, region_alpha, energy_grid, energy_index):
    level = jnp.sum(
        jnp.where(jnp.arange(energy_grid.shape[0]) == energy_index[0], energy_grid, 0.0)
    )
    onehot = (regions[:, :, None] == jnp.arange(region_mass.shape[0])[None, None, :]).astype(
        jnp.float32
    )
    per_region = region_mass * (1.0 + region_alpha * level)
    mass = jnp.sum(onehot * per_region[None, None, :], axis=2)
    return 2.0 / (mass[:-1] + mass[1:])


def on_device(left_inverse, regions, region_mass, region_alpha, energy_grid, energy_index):
    hop = couplings(regions, region_mass, region_alpha, energy_grid, energy_index)
    count = left_inverse.shape[0]
    own_rows = left_inverse.shape[2]
    offset = lax.axis_index("cols") * own_rows
    own_hop = lax.dynamic_slice_in_dim(hop, offset, own_rows, 1)
    scaled_all = (own_hop[:, None, :, None] * left_inverse[: count - 1].astype(jnp.float32)).astype(
        jnp.bfloat16
    )
    next_green = left_inverse[count - 1]
    blocks = []
    for index in range(count - 2, -1, -1):
        panel = left_inverse[index]
        factor = own_hop[index][None, :, None]
        columns = next_green
        product = complex_product(
            columns, lax.all_gather(scaled_all[index], "cols", axis=1, tiled=True)
        )
        image = (factor * product).astype(jnp.bfloat16)
        coupled = complex_product(panel, lax.all_gather(image, "cols", axis=1, tiled=True))
        current = panel.astype(jnp.float32) + coupled
        blocks.append(current)
        next_green = current.astype(jnp.bfloat16)
    return jnp.stack(blocks[::-1])


def solution(mesh):
    in_specs = (P("energy", None, "cols", None), P(), P(), P(), P(), P("energy"))
    out_specs = P("energy", None, "cols", None)
    return jax.shard_map(
        on_device, mesh=mesh, in_specs=in_specs, out_specs=out_specs, check_vma=False
    )
```

profile of v0, /device:TPU:1, one launch (start us, length us, event | category | flops | bytes accessed | tf_op | source)
XLA Modules:
  0.0 275.4 jit_solution(11490051664534645969)
XLA Ops:
  6.5 0.0 copy-start
  6.5 0.0 all-gather.11.cloned.1.call-start
  7.3 1.3 fusion.59
  8.6 1.3 add_multiply_fusion
  9.9 0.9 select_reduce_fusion
  10.8 0.1 fusion.58
  10.9 1.2 multiply_convert_fusion
  12.1 0.9 fusion.60
  13.0 0.0 all-gather.11.cloned.1.call-update
  13.0 0.0 all-gather.7.cloned.1.call-start
  13.0 58.8 %all-gather.11.cloned.1.call-done = bf16[1,2,1536,1536]{3,2,1,0:T(8,128)(2,1)} async-done(((bf16[1,2,48,1536]{3,2,1,0:T(8,128)(2,1)}), bf16[1,2,1536,1536]{3,2,1,0:T(8,128)(2,1)}) %all-gather.11.cloned.1.call-update) | async-done | bytes 9437200 | tf_op jit(solution)/shard_map/all_gather | solution.py:45
  71.8 0.0 copy-start.3
  71.8 3.5 %fusion = f32[1536,48]{0,1:T(8,128)S(1)} fusion(bf16[1,2,1536,1536]{3,2,1,0:T(8,128)(2,1)} %all-gather.11.cloned.1.call-done, bf16[3,2,48,1536]{3,2,1,0:T(8,128)(2,1)} %param.6), kind=kOutput, calls=%fused_computation.8 | convolution fusion | flops 226492416 | bytes 5160960 | tf_op jit(solution)/shard_map/dot_general | solution.py:8
  75.3 0.0 copy-done
  75.3 3.8 %fusion.1 = f32[1536,48]{0,1:T(8,128)S(1)} fusion(bf16[1,2,1536,1536]{3,2,1,0:T(8,128)(2,1)} %all-gather.11.cloned.1.call-done, bf16[3,2,48,1536]{3,2,1,0:T(8,128)(2,1)S(1)} %copy-done), kind=kOutput, calls=%fused_computation.9 | convolution fusion | flops 226492416 | bytes 5160960 | tf_op jit(solution)/shard_map/dot_general | solution.py:11
  79.1 0.0 copy-done.3
  79.2 0.9 fusion.24
  80.1 0.9 fusion.25
  81.0 0.8 fusion.32
  81.8 0.0 all-gather.7.cloned.1.call-update
  81.8 0.0 all-gather.13.cloned.1.call-start
  81.9 0.7 all-gather.13.cloned.1.call-update
  82.6 0.0 all-gather.9.cloned.1.call-start
  82.6 54.1 %all-gather.7.cloned.1.call-done = bf16[2,1536,1536]{2,1,0:T(8,128)(2,1)} async-done(((bf16[2,48,1536]{2,1,0:T(8,128)(2,1)}), bf16[2,1536,1536]{2,1,0:T(8,128)(2,1)}) %all-gather.7.cloned.1.call-update) | async-done | bytes 9437200 | tf_op jit(solution)/shard_map/all_gather | solution.py:48
  136.7 0.0 copy-start.2
  136.7 3.4 %fusion.4 = f32[1536,48]{0,1:T(8,128)S(1)} fusion(bf16[2,1536,1536]{2,1,0:T(8,128)(2,1)} %all-gather.7.cloned.1.call-done, bf16[3,2,48,1536]{3,2,1,0:T(8,128)(2,1)S(1)} %copy-done), kind=kOutput, calls=%fused_computation.12 | convolution fusion | flops 226492416 | bytes 5160960 | tf_op jit(solution)/shard_map/dot_general | solution.py:8
  140.1 3.9 %fusion.5 = f32[1536,48]{0,1:T(8,128)S(1)} fusion(bf16[2,1536,1536]{2,1,0:T(8,128)(2,1)} %all-gather.7.cloned.1.call-done, bf16[3,2,48,1536]{3,2,1,0:T(8,128)(2,1)S(1)} %copy-done), kind=kOutput, calls=%fused_computation.13 | convolution fusion | flops 226492416 | bytes 5160960 | tf_op jit(solution)/shard_map/dot_general | solution.py:11
  143.9 0.0 copy-done.2
  144.0 0.9 fusion.21
  144.9 0.9 fusion.20
  145.8 0.1 fusion.31
  145.9 47.8 %all-gather.13.cloned.1.call-done = bf16[1,2,1536,1536]{3,2,1,0:T(8,128)(2,1)} async-done(((bf16[1,2,48,1536]{3,2,1,0:T(8,128)(2,1)}), bf16[1,2,1536,1536]{3,2,1,0:T(8,128)(2,1)}) %all-gather.13.cloned.1.call-update) | async-done | bytes 9437200 | tf_op jit(solution)/shard_map/all_gather | solution.py:45
  193.7 0.0 copy-start.1
  193.7 3.4 %fusion.9 = f32[48,1536]{1,0:T(8,128)S(1)} fusion(bf16[1,2,1536,1536]{3,2,1,0:T(8,128)(2,1)} %all-gather.13.cloned.1.call-done, bf16[2,48,1536]{2,1,0:T(8,128)(2,1)S(1)} %fusion.31), kind=kOutput, calls=%fused_computation.17 | convolution fusion | flops 226492416 | bytes 5160960 | tf_op jit(solution)/shard_map/dot_general | solution.py:8
  197.1 3.9 %fusion.8 = f32[48,1536]{1,0:T(8,128)S(1)} fusion(bf16[1,2,1536,1536]{3,2,1,0:T(8,128)(2,1)} %all-gather.13.cloned.1.call-done, bf16[2,48,1536]{2,1,0:T(8,128)(2,1)S(1)} %fusion.31), kind=kOutput, calls=%fused_computation.16 | convolution fusion | flops 226492416 | bytes 5160960 | tf_op jit(solution)/shard_map/dot_general | solution.py:11
  201.0 0.0 copy-done.1
  201.0 0.9 fusion.27
  201.9 0.9 fusion.26
  202.8 0.8 fusion.33
  203.7 0.0 all-gather.9.cloned.1.call-update
  203.7 54.8 %all-gather.9.cloned.1.call-done = bf16[2,1536,1536]{2,1,0:T(8,128)(2,1)} async-done(((bf16[2,48,1536]{2,1,0:T(8,128)(2,1)}), bf16[2,1536,1536]{2,1,0:T(8,128)(2,1)}) %all-gather.9.cloned.1.call-update) | async-done | bytes 9437200 | tf_op jit(solution)/shard_map/all_gather | solution.py:48
  258.5 3.4 %fusion.12 = f32[1536,48]{0,1:T(8,128)S(1)} fusion(bf16[2,1536,1536]{2,1,0:T(8,128)(2,1)} %all-gather.9.cloned.1.call-done, bf16[3,2,48,1536]{3,2,1,0:T(8,128)(2,1)S(1)} %copy-done), kind=kOutput, calls=%fused_computation.20 | convolution fusion | flops 226492416 | bytes 5160960 | tf_op jit(solution)/shard_map/dot_general | solution.py:8
  261.9 3.9 %fusion.13 = f32[1536,48]{0,1:T(8,128)S(1)} fusion(bf16[2,1536,1536]{2,1,0:T(8,128)(2,1)} %all-gather.9.cloned.1.call-done, bf16[3,2,48,1536]{3,2,1,0:T(8,128)(2,1)S(1)} %copy-done), kind=kOutput, calls=%fused_computation.21 | convolution fusion | flops 226492416 | bytes 5160960 | tf_op jit(solution)/shard_map/dot_general | solution.py:11
  265.8 0.0 copy-done.4
  265.8 0.9 fusion.28
  266.7 0.9 fusion.29
  267.6 0.1 maximum_add_fusion
  267.8 1.1 pad_maximum_fusion
  (3 shorter events, 0.0 us)
Async XLA Ops:
  6.5 68.8 %copy-start = (bf16[3,2,48,1536]{3,2,1,0:T(8,128)(2,1)S(1)}, bf16[3,2,48,1536]{3,2,1,0:T(8,128)(2,1)}, u32[]{:S(2)}) copy-start(bf16[3,2,48,1536]{3,2,1,0:T(8,128)(2,1)} %param.6) | copy-start | bytes 2654212
  6.5 65.3 %all-gather.11.cloned.1.call-start = ((), (), s32[]{:S(2)}) async-start(), calls=%async_computation.2 | async-start | bytes 9732096 | tf_op jit(solution)/shard_map/all_gather | solution.py:45
  13.0 123.7 %all-gather.7.cloned.1.call-start = ((), (), s32[]{:S(2)}) async-start(), calls=%async_computation | async-start | bytes 9732096 | tf_op jit(solution)/shard_map/all_gather | solution.py:48
  71.8 7.3 %copy-start.3 = (bf16[1,2,1536,1536]{3,2,1,0:T(8,128)(2,1)S(1)}, bf16[1,2,1536,1536]{3,2,1,0:T(8,128)(2,1)}, u32[]{:S(2)}) copy-start(bf16[1,2,1536,1536]{3,2,1,0:T(8,128)(2,1)} %all-gather.11.cloned.1.call-done) | copy-start | bytes 28311556
  81.8 111.9 %all-gather.13.cloned.1.call-start = ((), (), s32[]{:S(2)}) async-start(), calls=%async_computation.3 | async-start | bytes 9732096 | tf_op jit(solution)/shard_map/all_gather | solution.py:45
  82.6 175.9 %all-gather.9.cloned.1.call-start = ((), (), s32[]{:S(2)}) async-start(), calls=%async_computation.1 | async-start | bytes 9732096 | tf_op jit(solution)/shard_map/all_gather | solution.py:48
  136.7 7.3 %copy-start.2 = (bf16[2,1536,1536]{2,1,0:T(8,128)(2,1)S(1)}, bf16[2,1536,1536]{2,1,0:T(8,128)(2,1)}, u32[]{:S(2)}) copy-start(bf16[2,1536,1536]{2,1,0:T(8,128)(2,1)} %all-gather.7.cloned.1.call-done) | copy-start | bytes 28311556
  193.7 7.3 %copy-start.1 = (bf16[1,2,1536,1536]{3,2,1,0:T(8,128)(2,1)S(1)}, bf16[1,2,1536,1536]{3,2,1,0:T(8,128)(2,1)}, u32[]{:S(2)}) copy-start(bf16[1,2,1536,1536]{3,2,1,0:T(8,128)(2,1)} %all-gather.13.cloned.1.call-done) | copy-start | bytes 28311556
  258.5 7.3 %copy-start.4 = (bf16[2,1536,1536]{2,1,0:T(8,128)(2,1)S(1)}, bf16[2,1536,1536]{2,1,0:T(8,128)(2,1)}, u32[]{:S(2)}) copy-start(bf16[2,1536,1536]{2,1,0:T(8,128)(2,1)} %all-gather.9.cloned.1.call-done) | copy-start | bytes 28311556
Sparse Core Ops, SparseCore 0:
  13.1 58.6 all-gather.10
  82.0 54.6 all-gather.6
  139.0 54.6 all-gather.12
  203.8 54.6 all-gather.8
where the time goes:
time: 276 us; the launch traced here: 275 us
  waiting for transfers between devices  216 us (78%)
  matrix products  36.3 us (13%)
  between operations  14 us (5%)
  other arithmetic  7.77 us (3%)
    all_gather x2, waiting for transfers between devices, on_device(): lax.all_gather(image, 'cols', axis=1, tiled=True)  109 us
    all_gather x2, waiting for transfers between devices, on_device(): lax.all_gather(scaled_all[index], 'cols', axis=1, tiled=True)  107 us
    dot_general x4, matrix products, complex_product(): jnp.dot(left[1], right[0], preferred_element_type=jnp.float32)  15.4 us
    dot_general x4, matrix products, complex_product(): jnp.dot(left[0], right[0], preferred_element_type=jnp.float32)  13.6 us
  transfers between devices with their start and end apart: 4, of which 4 were waited for; matrix products, arithmetic and copies ran while one was open for 3% of the time, Pallas kernels for 0%

commit v1 on v0

v1 whole, which is shorter than its diff:
```python
import functools

import jax
import jax.numpy as jnp
from jax import lax
from jax.experimental import pallas as pl
from jax.experimental.pallas import tpu as pltpu
from jax.sharding import PartitionSpec as P

SIDE = 4
CORES = 2
BF = jnp.bfloat16
F32 = jnp.float32


def dot(a, b):
    return lax.dot_general(a, b, (((1,), (0,)), ((), ())), preferred_element_type=F32)


def dot_t(a, b):
    return lax.dot_general(a, b, (((1,), (1,)), ((), ())), preferred_element_type=F32)


def complex_dot(ar, ai, br, bi, op):
    return op(ar, br) - op(ai, bi), op(ar, bi) + op(ai, br)


class Sems:
    def __init__(self, ref):
        self.ref = ref
        self.used = 0

    def take(self):
        self.used += 1
        return self.ref.at[self.used - 1]


class Gather:
    def __init__(self, me, device, source, slot, send, recv, sibling=None):
        self.me = me
        self.plus = lax.rem(me + 1, SIDE)
        self.minus = lax.rem(me + 3, SIDE)
        self.far = lax.rem(me + 2, SIDE)
        self.device, self.source, self.slot = device, source, slot
        self.send, self.recv = send, recv
        self.sibling = sibling
        self.copies = []
        self.sib = {}

    def remote(self, src, dst, device):
        copy = pltpu.make_async_remote_copy(
            src_ref=src,
            dst_ref=dst,
            send_sem=self.send.take(),
            recv_sem=self.recv.take(),
            device_id={"cols": device},
            device_id_type=pl.DeviceIdType.MESH,
        )
        copy.start()
        self.copies.append(copy)
        return copy

    def start(self):
        right, left = self.device(self.plus), self.device(self.minus)
        me = self.me
        self.r0 = self.remote(self.source(0), self.slot(me, 0), right)
        self.l1 = self.remote(self.source(1), self.slot(me, 1), left)
        self.r1 = self.remote(self.source(1), self.slot(me, 1), right)
        self.l0 = self.remote(self.source(0), self.slot(me, 0), left)
        if self.sibling is not None:
            for p in range(2):
                self.share("own", me, p, self.source(p))

    def share(self, name, slot, p, src=None):
        if self.sibling is None:
            return
        ref = self.slot(slot, p)
        self.sib[name, p] = self.remote(ref if src is None else src, ref, self.sibling)

    def forward(self):
        self.r0.wait_recv()
        self.fr = self.remote(self.slot(self.minus, 0), self.slot(self.minus, 0), self.device(self.plus))
        self.l1.wait_recv()
        self.fl = self.remote(self.slot(self.plus, 1), self.slot(self.plus, 1), self.device(self.minus))
        self.share("minus", self.minus, 0)
        self.share("plus", self.plus, 1)

    def near(self):
        self.r1.wait_recv()
        self.share("minus", self.minus, 1)
        self.l0.wait_recv()
        self.share("plus", self.plus, 0)

    def last(self):
        self.fr.wait_recv()
        self.share("far", self.far, 0)
        self.fl.wait_recv()
        self.share("far", self.far, 1)

    def sib_wait(self, name):
        if self.sibling is not None:
            for p in range(2):
                self.sib[name, p].wait_recv()

    def drain(self):
        for copy in self.copies:
            copy.wait_send()


def group_order(pieces):
    return jnp.concatenate([pieces[b][a] for a in range(SIDE) for b in range(SIDE)], axis=-1)


def exchanged(value, width):
    rows = [
        [value[:, (a * SIDE + b) * width : (a * SIDE + b + 1) * width] for b in range(SIDE)] for a in range(SIDE)
    ]
    return group_order(rows)


def kernel(
    left,
    regions,
    region_mass,
    region_alpha,
    energy_grid,
    energy_index,
    out,
    row2,
    row1,
    row0,
    col1,
    col0,
    scaled,
    mine0,
    image1,
    image0,
    green1,
    final,
    ends,
    acc,
    hop_t,
    pick,
    send_sems,
    recv_sems,
    local_sems,
):
    me = lax.axis_index("cols")
    c = lax.rem(me, CORES)
    j = lax.rem(me // CORES, SIDE)
    i = me // (CORES * SIDE)
    sibling = me + 1 - 2 * c

    def at(x, y):
        return (x * SIDE + y) * CORES + c

    def along_x(x):
        return at(x, j)

    def along_y(y):
        return at(i, y)

    rows = left.shape[2]
    size = left.shape[3]
    chip = CORES * rows
    panel = SIDE * chip
    high = SIDE * rows

    send, recv, local = Sems(send_sems), Sems(recv_sems), Sems(local_sems)

    barrier = pltpu.get_barrier_semaphore()
    peers = [sibling] + [along_x(lax.rem(i + s, SIDE)) for s in (1, 3)] + [along_y(lax.rem(j + s, SIDE)) for s in (1, 2, 3)]
    for peer in peers:
        pl.semaphore_signal(barrier, inc=1, device_id={"cols": peer}, device_id_type=pl.DeviceIdType.MESH)
    pl.semaphore_wait(barrier, len(peers))

    g_row2 = Gather(j, along_y, lambda p: left.at[2, p], lambda s, p: row2.at[p, s], send, recv)
    g_col1 = Gather(i, along_x, lambda p: left.at[1, p], lambda s, p: col1.at[p, s, c], send, recv, sibling)
    g_row1 = Gather(j, along_y, lambda p: left.at[1, p], lambda s, p: row1.at[p, s], send, recv)
    g_image1 = Gather(
        i, along_x, lambda p: image1.at[p, i, :, c], lambda s, p: image1.at[p, s, :, c], send, recv, sibling
    )
    g_green = Gather(j, along_y, lambda p: green1.at[p, j], lambda s, p: green1.at[p, s], send, recv)
    g_col0 = Gather(i, along_x, lambda p: mine0.at[p], lambda s, p: col0.at[p, s, c], send, recv, sibling)
    g_row0 = Gather(j, along_y, lambda p: left.at[0, p], lambda s, p: row0.at[p, s], send, recv)
    g_image0 = Gather(
        i, along_x, lambda p: image0.at[p, i, :, c], lambda s, p: image0.at[p, s, :, c], send, recv, sibling
    )

    g_row2.start()
    g_col1.start()
    locals_ = {}
    for name, src, dst in (
        ("row2", 2, lambda p: row2.at[p, j]),
        ("col1", 1, lambda p: col1.at[p, i, c]),
        ("row1", 1, lambda p: row1.at[p, j]),
        ("row0", 0, lambda p: row0.at[p, j]),
    ):
        locals_[name] = []
        for p in range(2):
            copy = pltpu.make_async_copy(left.at[src, p], dst(p), local.take())
            copy.start()
            locals_[name].append(copy)

    def local_wait(name):
        for copy in locals_[name]:
            copy.wait()

    level = jnp.float32(0.0)
    wanted = energy_index[0]
    for e in range(energy_grid.shape[0]):
        level = jnp.where(wanted == e, energy_grid[e], level)
    where = regions[...]
    mass = jnp.zeros(where.shape, F32)
    for r in range(region_mass.shape[0]):
        mass = jnp.where(where == r, region_mass[r] * (1.0 + region_alpha[r] * level), mass)
    hop0 = 2.0 / (mass[0:1] + mass[1:2])
    hop1 = 2.0 / (mass[1:2] + mass[2:3])
    for s, hop in enumerate((hop0, hop1)):
        for b in range(size // 128):
            tile = jnp.broadcast_to(hop[:, b * 128 : (b + 1) * 128], (128, 128))
            hop_t[s, b * 128 : (b + 1) * 128, :] = tile.T
    hop0_c = exchanged(hop0, chip)

    local_wait("row0")
    for p in range(2):
        mine0[p] = exchanged(row0[p, j].astype(F32), chip).astype(BF)

    for k in range(SIDE):
        n = lax.broadcasted_iota(jnp.int32, (panel, panel), 0)
        q = lax.broadcasted_iota(jnp.int32, (panel, panel), 1)
        keep = n + (k - j) * chip == q
        keep = keep & (q >= k * chip) & (q < (k + 1) * chip)
        pick[k * panel : (k + 1) * panel, :] = jnp.where(keep, 1.0, 0.0).astype(BF)

    def scale_block(col, slot, core, hop):
        for p in range(2):
            start = pl.multiple_of((slot * CORES + core) * rows, 16)
            scaled[p, pl.ds(start, rows), :] = (col[p, slot, core].astype(F32) * hop).astype(BF)

    def scale_own(col, slot, hop):
        scale_block(col, slot, c, hop)

    def scale_sib(g, name, col, slot, hop):
        g.sib_wait(name)
        scale_block(col, slot, 1 - c, hop)

    def store_image(image, s, real, imag):
        for m in range(SIDE):
            start = pl.multiple_of(i * panel + m * chip + c * rows, 16)
            h = hop_t[s, pl.ds(start, rows), :]
            h = jnp.concatenate([h] * (panel // 128), axis=1)
            part = slice(m * rows, (m + 1) * rows)
            image[0, i, m, c] = (h * real[part]).astype(BF)
            image[1, i, m, c] = (h * imag[part]).astype(BF)

    def init_acc(row):
        for p in range(2):
            acc[p] = dot(row[p].reshape(high, size), pick[...])

    def add_chunk(row, image, k):
        lanes = pl.ds(pl.multiple_of(k * panel, 128), panel)
        ar, ai = (row[p, :, :, lanes].reshape(high, panel) for p in range(2))
        br, bi = (image[p, k].reshape(panel, panel) for p in range(2))
        real, imag = complex_dot(ar, ai, br, bi, dot)
        acc[0] += real
        acc[1] += imag

    g_row2.forward()
    g_col1.forward()
    g_row1.start()
    local_wait("col1")
    scale_own(col1, i, hop1)
    scale_sib(g_col1, "own", col1, i, hop1)
    g_col1.near()
    g_row2.near()
    scale_own(col1, g_col1.minus, hop1)
    scale_own(col1, g_col1.plus, hop1)
    scale_sib(g_col1, "minus", col1, g_col1.minus, hop1)
    scale_sib(g_col1, "plus", col1, g_col1.plus, hop1)
    local_wait("row2")
    g_col1.last()
    g_row2.last()
    scale_own(col1, g_col1.far, hop1)
    scale_sib(g_col1, "far", col1, g_col1.far, hop1)

    ar, ai = (row2[p].reshape(high, size) for p in range(2))
    real, imag = complex_dot(ar, ai, scaled[0], scaled[1], dot_t)
    store_image(image1, 1, real, imag)
    g_image1.start()

    g_row1.forward()
    local_wait("row1")
    g_row1.near()
    g_image1.forward()
    g_col0.start()
    g_image1.near()
    g_row1.last()
    init_acc(row1)
    g_image1.sib_wait("own")
    add_chunk(row1, image1, i)
    for name, slot in (("minus", g_image1.minus), ("plus", g_image1.plus)):
        g_image1.sib_wait(name)
        add_chunk(row1, image1, slot)
    g_image1.last()
    g_image1.sib_wait("far")
    add_chunk(row1, image1, g_image1.far)
    for p in range(2):
        green1[p, j] = acc[p].astype(BF)
    g_green.start()

    g_col0.forward()
    g_col0.near()
    g_green.forward()
    g_row0.start()

    def scale_col0(name, slot):
        if name != "own":
            scale_own(col0, slot, hop0_c)
        scale_sib(g_col0, name, col0, slot, hop0_c)

    for p in range(2):
        start = pl.multiple_of((i * CORES + c) * rows, 16)
        scaled[p, pl.ds(start, rows), :] = (mine0[p].astype(F32) * hop0_c).astype(BF)
    scale_col0("own", i)
    scale_col0("minus", g_col0.minus)
    scale_col0("plus", g_col0.plus)
    g_col0.last()
    scale_col0("far", g_col0.far)

    def green_chunk(m, first=False):
        lanes = pl.ds(pl.multiple_of(m * panel, 128), panel)
        real, imag = complex_dot(green1[0, m], green1[1, m], scaled[0, :, lanes], scaled[1, :, lanes], dot_t)
        if first:
            acc[0] = real
            acc[1] = imag
        else:
            acc[0] += real
            acc[1] += imag

    green_chunk(j, True)
    g_green.near()
    green_chunk(g_green.minus)
    green_chunk(g_green.plus)
    g_green.last()
    green_chunk(g_green.far)
    store_image(image0, 0, acc[0], acc[1])
    g_image0.start()

    g_row0.forward()
    mine = pl.ds(pl.multiple_of(j * rows, 16), rows)
    for p in range(2):
        whole = jnp.concatenate([green1[p, m, mine, :].astype(F32) for m in range(SIDE)], axis=1)
        out[1, p] = exchanged(whole, chip)
    g_row0.near()
    g_image0.forward()
    g_image0.near()
    g_row0.last()
    init_acc(row0)
    g_image0.sib_wait("own")
    add_chunk(row0, image0, i)
    for name, slot in (("minus", g_image0.minus), ("plus", g_image0.plus)):
        g_image0.sib_wait(name)
        add_chunk(row0, image0, slot)
    g_image0.last()
    g_image0.sib_wait("far")
    add_chunk(row0, image0, g_image0.far)

    for m in range(SIDE):
        for p in range(2):
            ends[m, p] = acc[p, m * rows : (m + 1) * rows, :].astype(BF)
    tail = []
    for shift in (2, 1, 3):
        to = lax.rem(j + shift, SIDE)
        copy = pltpu.make_async_remote_copy(
            src_ref=ends.at[to],
            dst_ref=final.at[j],
            send_sem=send.take(),
            recv_sem=recv.take(),
            device_id={"cols": along_y(to)},
            device_id_type=pl.DeviceIdType.MESH,
        )
        copy.start()
        tail.append(copy)
    final[j] = ends[j]
    for copy in tail:
        copy.wait_recv()
    for p in range(2):
        whole = jnp.concatenate([final[m, p].astype(F32) for m in range(SIDE)], axis=1)
        out[0, p] = exchanged(whole, chip)
    for g in (g_row2, g_col1, g_row1, g_image1, g_green, g_col0, g_row0, g_image0):
        g.drain()
    for copy in tail:
        copy.wait_send()


def on_device(left_inverse, regions, region_mass, region_alpha, energy_grid, energy_index):
    count, _, rows, size = left_inverse.shape
    high, panel = SIDE * rows, SIDE * CORES * rows
    vmem = pl.BlockSpec(memory_space=pltpu.VMEM)
    smem = pl.BlockSpec(memory_space=pltpu.SMEM)
    copies = 4 * 6 + 4 * 14 + 3
    return pl.pallas_call(
        kernel,
        out_shape=jax.ShapeDtypeStruct((count - 1, 2, rows, size), F32),
        in_specs=[pl.BlockSpec(memory_space=pl.ANY), vmem, smem, smem, smem, smem],
        out_specs=vmem,
        scratch_shapes=[
            pltpu.VMEM((2, SIDE, rows, size), BF),
            pltpu.VMEM((2, SIDE, rows, size), BF),
            pltpu.VMEM((2, SIDE, rows, size), BF),
            pltpu.VMEM((2, SIDE, CORES, rows, size), BF),
            pltpu.VMEM((2, SIDE, CORES, rows, size), BF),
            pltpu.VMEM((2, panel, size), BF),
            pltpu.VMEM((2, rows, size), BF),
            pltpu.VMEM((2, SIDE, SIDE, CORES, rows, panel), BF),
            pltpu.VMEM((2, SIDE, SIDE, CORES, rows, panel), BF),
            pltpu.VMEM((2, SIDE, high, panel), BF),
            pltpu.VMEM((SIDE, 2, rows, panel), BF),
            pltpu.VMEM((SIDE, 2, rows, panel), BF),
            pltpu.VMEM((2, high, panel), F32),
            pltpu.VMEM((2, size, 128), F32),
            pltpu.VMEM((size, panel), BF),
            pltpu.SemaphoreType.DMA((copies,)),
            pltpu.SemaphoreType.DMA((copies,)),
            pltpu.SemaphoreType.DMA((8,)),
        ],
        compiler_params=pltpu.CompilerParams(
            collective_id=0, has_side_effects=True, vmem_limit_bytes=60 * 1024 * 1024
        ),
    )(left_inverse, regions, region_mass, region_alpha, energy_grid, energy_index)


def solution(mesh):
    in_specs = (P("energy", None, "cols", None), P(), P(), P(), P(), P("energy"))
    out_specs = P("energy", None, "cols", None)
    return jax.shard_map(
        on_device, mesh=mesh, in_specs=in_specs, out_specs=out_specs, check_vma=False
    )
```

time: 276 us -> 73.2 us (0.27)
  waiting for transfers between devices: 216 us -> 0 us
  Pallas kernels: 0 us -> 69.9 us
  matrix products: 36.3 us -> 0 us
  between operations: 14 us -> 0.66 us
  other arithmetic: 7.77 us -> 0 us
    all_gather x4 -> x0, waiting for transfers between devices: 216 us -> none  [the longest x2 109 us: on_device(): lax.all_gather(image, 'cols', axis=1, tiled=True)]
    pallas_call x0 -> x1, Pallas kernels: none -> 69.9 us  [on_device(): pl.pallas_call(kernel, out_shape=jax.ShapeDtypeStruct((count - 1, 2, rows...]
    dot_general x16 -> x0, matrix products: 36.3 us -> none  [the longest x4 15.4 us: complex_product(): jnp.dot(left[1], right[0], preferred_element_type=jnp.float32)]
    convert_element_type x4 -> x0, other arithmetic: 2.95 us -> none  [the longest x2 1.64 us: on_device(): image = (factor * product).astype(jnp.bfloat16)]
  transfers between devices with their start and end apart: 4 -> 0, of which waited for: 4 -> 0; matrix products, arithmetic and copies ran while one was open for 3% -> 0% of each run, Pallas kernels for 0% -> 0%
where the time goes in v1:
time: 73.2 us; the launch traced here: 72.9 us
  Pallas kernels  69.9 us (95%)
  local copies, waits for them, and re-layouts  2.36 us (3%)
    pallas_call x1, Pallas kernels, on_device(): pl.pallas_call(kernel, out_shape=jax.ShapeDtypeStruct((count - 1, 2, rows...  69.9 us
    unnamed x1, local copies, waits for them, and re-layouts  2.36 us

profile of v1, /device:TPU:1, one launch (start us, length us, event | category | flops | bytes accessed | tf_op | source)
XLA Modules:
  0.0 72.9 jit_solution(17575569359132384889)
XLA Ops:
  0.7 69.9 %shard_map.64 = f32[2,2,48,1536]{3,2,1,0:T(8,128)} custom-call(bf16[3,2,48,1536]{3,2,1,0:T(8,128)(2,1)} %left.1, s32[3,1536]{1,0:T(4,128)} %regions.1, f32[3]{0:T(128)} %region_mass.1, f32[3]{0:T(128)} %region_alpha.1, f32[16]{0:T(128)} %energy_grid.1, s32[1]{0:T(128)S(6)} %copy.8.energy_index), custom_call_target="tpu_custom_call" | custom-call | tf_op jit(solution)/shard_map/pallas_call | solution.py:403
  70.6 2.4 %copy.9 = f32[2,2,48,1536]{3,2,1,0:T(8,128)} copy(f32[2,2,48,1536]{3,2,1,0:T(8,128)} %shard_map.64) | data formatting | bytes 2359296

commit v2 on v0

v2 whole, which is shorter than its diff:
```python
import jax
import jax.numpy as jnp
from jax import lax
from jax.experimental import pallas as pl
from jax.experimental.pallas import tpu as pltpu
from jax.sharding import PartitionSpec as P

SIDE = 4
CORES = 2
BF = jnp.bfloat16
F32 = jnp.float32


def dot(a, b):
    return lax.dot_general(a, b, (((1,), (0,)), ((), ())), preferred_element_type=F32)


def dot_t(a, b):
    return lax.dot_general(a, b, (((1,), (1,)), ((), ())), preferred_element_type=F32)


class Sems:
    def __init__(self, ref):
        self.ref = ref
        self.used = 0

    def take(self):
        self.used += 1
        return self.ref.at[self.used - 1]


class Remote:
    def __init__(self, copy):
        self.copy = copy
        self.left = False

    def wait_recv(self):
        self.copy.wait_recv()

    def wait_send(self):
        if not self.left:
            self.left = True
            self.copy.wait_send()


class Gather:
    def __init__(self, me, device, source, slot, send, recv, sibling=None, parts=1):
        self.me = me
        self.plus = lax.rem(me + 1, SIDE)
        self.minus = lax.rem(me + 3, SIDE)
        self.far = lax.rem(me + 2, SIDE)
        self.right, self.left = device(self.plus), device(self.minus)
        self.source, self.slot = source, slot
        self.send, self.recv = send, recv
        self.sibling = sibling
        self.parts = parts
        self.copies = []
        self.sib = {"own": [], "minus": [], "plus": [], "far": []}

    def remote(self, src, dst, device):
        copy = pltpu.make_async_remote_copy(
            src_ref=src,
            dst_ref=dst,
            send_sem=self.send.take(),
            recv_sem=self.recv.take(),
            device_id={"cols": device},
            device_id_type=pl.DeviceIdType.MESH,
        )
        copy.start()
        copy = Remote(copy)
        self.copies.append(copy)
        return copy

    def cut(self, ref, q):
        if self.parts == 1:
            return ref
        n = ref.shape[0] // self.parts
        return ref.at[q * n : (q + 1) * n]

    def first(self):
        self.r0 = self.remote(self.source(0), self.slot(self.me, 0), self.right)
        self.l1 = self.remote(self.source(1), self.slot(self.me, 1), self.left)

    def second(self):
        self.r1 = self.remote(self.source(1), self.slot(self.me, 1), self.right)
        self.l0 = self.remote(self.source(0), self.slot(self.me, 0), self.left)
        if self.sibling is not None:
            for p in range(2):
                self.share("own", self.source(p), self.slot(self.me, p))

    def sent(self):
        self.r0.wait_send()
        self.l1.wait_send()

    def share(self, name, src, dst):
        if self.sibling is not None:
            self.sib[name].append(self.remote(src, dst, self.sibling))

    def share_slot(self, name, ref):
        self.share(name, ref, ref)

    def forward(self):
        self.r0.wait_recv()
        ref = self.slot(self.minus, 0)
        self.fr = [self.remote(self.cut(ref, q), self.cut(ref, q), self.right) for q in range(self.parts)]
        self.l1.wait_recv()
        ref = self.slot(self.plus, 1)
        self.fl = [self.remote(self.cut(ref, q), self.cut(ref, q), self.left) for q in range(self.parts)]
        self.share_slot("minus", self.slot(self.minus, 0))
        self.share_slot("plus", self.slot(self.plus, 1))

    def passed_on(self):
        for copy in self.fr + self.fl:
            copy.wait_send()

    def near(self):
        self.r1.wait_recv()
        self.share_slot("minus", self.slot(self.minus, 1))
        self.l0.wait_recv()
        self.share_slot("plus", self.slot(self.plus, 0))

    def last(self):
        for q in range(self.parts):
            self.fr[q].wait_recv()
            self.share_slot("far", self.cut(self.slot(self.far, 0), q))
            self.fl[q].wait_recv()
            self.share_slot("far", self.cut(self.slot(self.far, 1), q))

    def sib_wait(self):
        for name in ("own", "minus", "plus", "far"):
            for copy in self.sib[name]:
                copy.wait_recv()

    def drain(self):
        for copy in self.copies:
            copy.wait_send()


def kernel(
    left,
    regions,
    region_mass,
    region_alpha,
    energy_grid,
    energy_index,
    out,
    row2,
    row1,
    row0,
    col1,
    col0,
    scaled1,
    scaled0,
    image1,
    image0,
    green,
    ends,
    final,
    acc,
    own1,
    hops,
    send_sems,
    recv_sems,
    local_sems,
    end_send,
    end_recv,
):
    me = lax.axis_index("cols")
    c = lax.rem(me, CORES)
    j = lax.rem(me // CORES, SIDE)
    i = me // (CORES * SIDE)
    sibling = me + 1 - 2 * c

    def along_x(x):
        return (x * SIDE + j) * CORES + c

    def along_y(y):
        return (i * SIDE + y) * CORES + c

    rows = left.shape[2]
    size = left.shape[3]
    panel = SIDE * CORES * rows
    half = 2 * rows
    here = pl.ds(pl.multiple_of(i * panel, 128), panel)

    def lanes(k):
        if isinstance(k, int):
            return slice(k * panel, (k + 1) * panel)
        return pl.ds(pl.multiple_of(k * panel, 128), panel)

    send, recv, local = Sems(send_sems), Sems(recv_sems), Sems(local_sems)

    barrier = pltpu.get_barrier_semaphore()
    peers = [sibling]
    peers += [along_x(lax.rem(i + s, SIDE)) for s in (1, 2, 3)]
    peers += [along_y(lax.rem(j + s, SIDE)) for s in (1, 3)]
    for peer in peers:
        pl.semaphore_signal(barrier, inc=1, device_id={"cols": peer}, device_id_type=pl.DeviceIdType.MESH)
    pl.semaphore_wait(barrier, len(peers))

    def rows_gather(s, row, parts):
        return Gather(j, along_y, lambda p: left.at[s, p], lambda m, p: row.at[p, m, c], send, recv, sibling, parts)

    def cols_gather(s, col):
        return Gather(i, along_x, lambda p: left.at[s, p], lambda k, p: col.at[p, k], send, recv)

    def image_gather(image, h):
        return Gather(i, along_x, lambda p: image.at[h, i, p], lambda k, p: image.at[h, k, p], send, recv)

    def green_gather(s):
        return Gather(
            j, along_y, lambda p: green.at[p, s, j, c], lambda m, p: green.at[p, s, m, c], send, recv, sibling
        )

    g_row2 = rows_gather(2, row2, 1)
    g_col1 = cols_gather(1, col1)
    g_row1 = rows_gather(1, row1, 1)
    g_col0 = cols_gather(0, col0)
    g_row0 = rows_gather(0, row0, 1)
    g_b = [image_gather(image1, h) for h in range(2)]
    g_c = [green_gather(s) for s in range(SIDE)]
    g_d = [image_gather(image0, s) for s in range(SIDE)]

    g_row2.first()
    g_col1.first()
    locals_ = {}
    for name, s, dst in (
        ("col1", 1, lambda p: col1.at[p, i]),
        ("row2", 2, lambda p: row2.at[p, j, c]),
        ("row1", 1, lambda p: row1.at[p, j, c]),
        ("col0", 0, lambda p: col0.at[p, i]),
        ("row0", 0, lambda p: row0.at[p, j, c]),
    ):
        locals_[name] = []
        for p in range(2):
            copy = pltpu.make_async_copy(left.at[s, p], dst(p), local.take())
            copy.start()
            locals_[name].append(copy)

    def local_wait(name):
        for copy in locals_[name]:
            copy.wait()

    level = jnp.float32(0.0)
    wanted = energy_index[0]
    for e in range(energy_grid.shape[0]):
        level = jnp.where(wanted == e, energy_grid[e], level)
    where = regions[...]
    mass = jnp.zeros(where.shape, F32)
    for r in range(region_mass.shape[0]):
        mass = jnp.where(where == r, region_mass[r] * (1.0 + region_alpha[r] * level), mass)
    hops[0:1] = 2.0 / (mass[0:1] + mass[1:2])
    hops[1:2] = 2.0 / (mass[1:2] + mass[2:3])

    def scale1(k):
        first = pl.multiple_of(lax.rem(k, 2) * rows, 16)
        for p in range(2):
            scaled1[k // 2, p, pl.ds(first, rows), :] = (col1[p, k].astype(F32) * hops[1:2]).astype(BF)

    def scale0(k):
        first = pl.multiple_of(k * rows, 16)
        for p in range(2):
            scaled0[p, pl.ds(first, rows), :] = (col0[p, k].astype(F32) * hops[0:1]).astype(BF)

    def whole(row, p):
        return row[p].reshape(panel, size)

    def chunk(row, p, k):
        return row[p, :, :, :, lanes(k)].reshape(panel, panel)

    g_row2.sent()
    g_row2.second()
    g_col1.sent()
    g_col1.second()
    local_wait("col1")
    scale1(i)
    g_row2.forward()
    g_col1.forward()
    g_row2.near()
    g_col1.near()
    g_row2.passed_on()
    g_row1.first()
    g_col1.passed_on()
    g_col0.first()
    scale1(g_col1.minus)
    scale1(g_col1.plus)
    local_wait("row2")
    g_row2.last()
    g_col1.last()
    scale1(g_col1.far)
    g_row1.sent()
    g_row1.second()
    g_row2.sib_wait()

    def first_image(h):
        a = scaled1[h].reshape(2 * half, size)
        re, im = dot_t(a, whole(row2, 0)), dot_t(a, whole(row2, 1))
        hop = hops[1:2, here]
        image1[h, i, 0] = (hop * (re[:half] - im[half:])).astype(BF)
        image1[h, i, 1] = (hop * (im[:half] + re[half:])).astype(BF)

    first_image(0)
    g_b[0].first()
    g_row1.forward()
    first_image(1)
    g_b[1].first()

    def add(image, row, h, k, start, count, init):
        a = image[h, k].reshape(2 * count, panel)
        for p in range(2):
            value = dot_t(a, chunk(row, p, k))
            if init:
                acc[p, start : start + 2 * count, :] = value
            else:
                acc[p, start : start + 2 * count, :] += value

    def planes(start, count):
        re, im = acc[0, start : start + 2 * count, :], acc[1, start : start + 2 * count, :]
        return re[:count] - im[count:], im[:count] + re[count:]

    g_row1.near()
    for h in range(2):
        g_b[h].sent()
        g_b[h].second()
    g_row1.passed_on()
    g_row0.first()
    for h in range(2):
        g_b[h].forward()
    local_wait("row1")
    g_row1.last()
    g_b[0].near()
    g_row1.sib_wait()
    for h in range(2):
        if h:
            g_b[h].near()
        start = h * 2 * half
        add(image1, row1, h, i, start, half, True)
        add(image1, row1, h, g_b[h].minus, start, half, False)
        add(image1, row1, h, g_b[h].plus, start, half, False)
        g_b[h].last()
        add(image1, row1, h, g_b[h].far, start, half, False)
        values = planes(start, half)
        for t in range(2):
            k = 2 * h + t
            for p in range(2):
                value = col1[p, k, :, here].astype(F32) + values[p][t * rows : (t + 1) * rows]
                green[p, k, j, c] = value.astype(BF)
                own1[p, k * rows : (k + 1) * rows, :] = value
            g_c[k].first()

    g_col0.second()
    g_col0.forward()
    local_wait("col0")
    scale0(i)
    for s in range(SIDE):
        g_c[s].sent()
        g_c[s].second()
    for s in range(SIDE):
        g_c[s].forward()
    g_col0.near()
    scale0(g_col0.minus)
    scale0(g_col0.plus)
    for s in range(SIDE):
        g_c[s].near()
    g_col0.last()
    scale0(g_col0.far)
    for s in range(SIDE):
        g_c[s].passed_on()
    g_row0.second()
    g_row0.forward()
    for s in range(SIDE):
        g_c[s].last()
    for s in range(SIDE):
        g_c[s].sib_wait()
        a = scaled0[:, :, lanes(s)].reshape(2 * SIDE * rows, panel)
        for p in range(2):
            value = dot(a, green[p, s].reshape(panel, panel))
            if s:
                acc[p] += value
            else:
                acc[p] = value
    high = SIDE * rows
    hop = hops[0:1, here]
    for s in range(SIDE):
        a, b = slice(s * rows, (s + 1) * rows), slice(high + s * rows, high + (s + 1) * rows)
        image0[s, i, 0] = (hop * (acc[0, a, :] - acc[1, b, :])).astype(BF)
        image0[s, i, 1] = (hop * (acc[1, a, :] + acc[0, b, :])).astype(BF)
        g_d[s].first()

    r = lax.broadcasted_iota(jnp.int32, (rows, panel), 0)
    q = lax.broadcasted_iota(jnp.int32, (rows, panel), 1)
    pick = jnp.where(q == r + (j * CORES + c) * rows, 1.0, 0.0).astype(BF)
    mine = pl.ds(pl.multiple_of(i * rows, 8), rows)
    for p in range(2):
        for k in range(SIDE):
            out[1, p, :, lanes(k)] = dot_t(pick, green[p, k].reshape(panel, panel))
        out[1, p, :, here] = own1[p, mine, :]
    for s in range(SIDE):
        g_d[s].sent()
        g_d[s].second()
    for s in range(SIDE):
        g_d[s].forward()
    g_row0.near()
    local_wait("row0")
    g_row0.last()
    g_row0.sib_wait()
    for s in range(SIDE):
        start = s * 2 * rows
        add(image0, row0, s, i, start, rows, True)
        g_d[s].near()
        add(image0, row0, s, g_d[s].minus, start, rows, False)
        add(image0, row0, s, g_d[s].plus, start, rows, False)

    def end(s, d):
        return pltpu.make_async_remote_copy(
            src_ref=ends.at[s],
            dst_ref=final.at[i],
            send_sem=end_send.at[d],
            recv_sem=end_recv.at[d],
            device_id={"cols": along_x(s)},
            device_id_type=pl.DeviceIdType.MESH,
        )

    for s in range(SIDE):
        start = s * 2 * rows
        g_d[s].last()
        add(image0, row0, s, g_d[s].far, start, rows, False)
        values = planes(start, rows)
        for p in range(2):
            value = col0[p, s, :, here].astype(F32) + values[p]
            ends[s, p] = value.astype(BF)
            own1[p, s * rows : (s + 1) * rows, :] = value

        @pl.when(i != s)
        def _():
            end(s, lax.rem(s - i + SIDE, SIDE)).start()

    final[i] = ends[i]
    for d in range(1, SIDE):
        end(lax.rem(i + d, SIDE), d).wait_recv()
    for p in range(2):
        for k in range(SIDE):
            out[0, p, :, lanes(k)] = final[k, p].astype(F32)
        out[0, p, :, here] = own1[p, mine, :]
    for g in [g_row2, g_col1, g_row1, g_col0, g_row0] + g_b + g_c + g_d:
        g.drain()
    for d in range(1, SIDE):
        end(lax.rem(i + d, SIDE), d).wait_send()


def on_device(left_inverse, regions, region_mass, region_alpha, energy_grid, energy_index):
    arrays = (left_inverse, regions, region_mass, region_alpha, energy_grid, energy_index)
    count, _, rows, size = left_inverse.shape
    panel = SIDE * CORES * rows
    vmem = pl.BlockSpec(memory_space=pltpu.VMEM)
    smem = pl.BlockSpec(memory_space=pltpu.SMEM)
    copies = 3 * 14 + 2 * 6 + 2 * 6 + 4 * 14 + 4 * 6
    return pl.pallas_call(
        kernel,
        out_shape=jax.ShapeDtypeStruct((count - 1, 2, rows, size), F32),
        in_specs=[pl.BlockSpec(memory_space=pl.ANY), vmem, smem, smem, smem, smem],
        out_specs=vmem,
        scratch_shapes=[
            pltpu.VMEM((2, SIDE, CORES, rows, size), BF),
            pltpu.VMEM((2, SIDE, CORES, rows, size), BF),
            pltpu.VMEM((2, SIDE, CORES, rows, size), BF),
            pltpu.VMEM((2, SIDE, rows, size), BF),
            pltpu.VMEM((2, SIDE, rows, size), BF),
            pltpu.VMEM((2, 2, 2 * rows, size), BF),
            pltpu.VMEM((2, SIDE * rows, size), BF),
            pltpu.VMEM((2, SIDE, 2, 2 * rows, panel), BF),
            pltpu.VMEM((SIDE, SIDE, 2, rows, panel), BF),
            pltpu.VMEM((2, SIDE, SIDE, CORES, rows, panel), BF),
            pltpu.VMEM((SIDE, 2, rows, panel), BF),
            pltpu.VMEM((SIDE, 2, rows, panel), BF),
            pltpu.VMEM((2, panel, panel), F32),
            pltpu.VMEM((2, SIDE * rows, panel), F32),
            pltpu.VMEM((2, size), F32),
            pltpu.SemaphoreType.DMA((copies,)),
            pltpu.SemaphoreType.DMA((copies,)),
            pltpu.SemaphoreType.DMA((10,)),
            pltpu.SemaphoreType.DMA((SIDE,)),
            pltpu.SemaphoreType.DMA((SIDE,)),
        ],
        compiler_params=pltpu.CompilerParams(
            collective_id=0, has_side_effects=True, vmem_limit_bytes=40 * 1024 * 1024
        ),
    )(*(pltpu.with_memory_space_constraint(x, pltpu.HBM) for x in arrays[:5]), energy_index)


def solution(mesh):
    in_specs = (P("energy", None, "cols", None), P(), P(), P(), P(), P("energy"))
    out_specs = P("energy", None, "cols", None)
    return jax.shard_map(
        on_device, mesh=mesh, in_specs=in_specs, out_specs=out_specs, check_vma=False
    )
```

time: 276 us -> 68 us (0.25)
  waiting for transfers between devices: 216 us -> 0 us
  Pallas kernels: 0 us -> 66.1 us
  matrix products: 36.3 us -> 0 us
  between operations: 14 us -> 0.66 us
  other arithmetic: 7.77 us -> 0 us
    all_gather x4 -> x0, waiting for transfers between devices: 216 us -> none  [the longest x2 109 us: on_device(): lax.all_gather(image, 'cols', axis=1, tiled=True)]
    pallas_call x0 -> x1, Pallas kernels: none -> 66.1 us  [on_device(): pl.pallas_call(kernel, out_shape=jax.ShapeDtypeStruct((count - 1, 2, rows...]
    dot_general x16 -> x0, matrix products: 36.3 us -> none  [the longest x4 15.4 us: complex_product(): jnp.dot(left[1], right[0], preferred_element_type=jnp.float32)]
    convert_element_type x4 -> x0, other arithmetic: 2.95 us -> none  [the longest x2 1.64 us: on_device(): image = (factor * product).astype(jnp.bfloat16)]
  transfers between devices with their start and end apart: 4 -> 0, of which waited for: 4 -> 0; matrix products, arithmetic and copies ran while one was open for 3% -> 0% of each run, Pallas kernels for 0% -> 0%
where the time goes in v2:
time: 68 us; the launch traced here: 67.8 us
  Pallas kernels  66.1 us (97%)
  local copies, waits for them, and re-layouts  1.02 us (2%)
    pallas_call x1, Pallas kernels, on_device(): pl.pallas_call(kernel, out_shape=jax.ShapeDtypeStruct((count - 1, 2, rows...  66.1 us

profile of v2, /device:TPU:1, one launch (start us, length us, event | category | flops | bytes accessed | tf_op | source)
XLA Modules:
  0.0 67.8 jit_solution(4555011150588207067)
XLA Ops:
  0.7 66.1 %shard_map.64 = f32[2,2,48,1536]{3,2,1,0:T(8,128)S(1)} custom-call(bf16[3,2,48,1536]{3,2,1,0:T(8,128)(2,1)} %left.1, s32[3,1536]{1,0:T(4,128)} %regions.1, f32[3]{0:T(128)} %region_mass.1, f32[3]{0:T(128)} %region_alpha.1, f32[16]{0:T(128)} %energy_grid.1, s32[1]{0:T(128)S(6)} %copy.8.energy_index), custom_call_target="tpu_custom_call" | custom-call | tf_op jit(solution)/shard_map/pallas_call | solution.py:458
  66.8 1.0 %copy.9 = f32[2,2,48,1536]{3,2,1,0:T(8,128)} copy(f32[2,2,48,1536]{3,2,1,0:T(8,128)S(1)} %shard_map.64) | data formatting | bytes 2359296

commit v3 on v1

--- a/solution.py
+++ b/solution.py
@@ -120,10 +120,10 @@
 
 def kernel(
     left,
-    regions,
-    region_mass,
-    region_alpha,
-    energy_grid,
+    regions_in,
+    region_mass_in,
+    region_alpha_in,
+    energy_grid_in,
     energy_index,
     out,
     row2,
@@ -144,6 +144,12 @@
     send_sems,
     recv_sems,
     local_sems,
+    own1,
+    regions,
+    region_mass,
+    region_alpha,
+    energy_grid,
+    small_sems,
 ):
     me = lax.axis_index("cols")
     c = lax.rem(me, CORES)
@@ -172,6 +178,15 @@
     peers = [sibling] + [along_x(lax.rem(i + s, SIDE)) for s in (1, 3)] + [along_y(lax.rem(j + s, SIDE)) for s in (1, 2, 3)]
     for peer in peers:
         pl.semaphore_signal(barrier, inc=1, device_id={"cols": peer}, device_id_type=pl.DeviceIdType.MESH)
+    small = []
+    for src, dst in (
+        (regions_in, regions),
+        (region_mass_in, region_mass),
+        (region_alpha_in, region_alpha),
+        (energy_grid_in, energy_grid),
+    ):
+        small.append(pltpu.make_async_copy(src, dst, small_sems.at[len(small)]))
+        small[-1].start()
     pl.semaphore_wait(barrier, len(peers))
 
     g_row2 = Gather(j, along_y, lambda p: left.at[2, p], lambda s, p: row2.at[p, s], send, recv)
@@ -206,6 +221,8 @@
         for copy in locals_[name]:
             copy.wait()
 
+    for copy in small:
+        copy.wait()
     level = jnp.float32(0.0)
     wanted = energy_index[0]
     for e in range(energy_grid.shape[0]):
@@ -305,9 +322,12 @@
     g_image1.last()
     g_image1.sib_wait("far")
     add_chunk(row1, image1, g_image1.far)
+    mine = pl.ds(pl.multiple_of(j * rows, 16), rows)
     for p in range(2):
         green1[p, j] = acc[p].astype(BF)
     g_green.start()
+    for p in range(2):
+        own1[p] = acc[p, mine, :]
 
     g_col0.forward()
     g_col0.near()
@@ -348,9 +368,9 @@
     g_image0.start()
 
     g_row0.forward()
-    mine = pl.ds(pl.multiple_of(j * rows, 16), rows)
-    for p in range(2):
-        whole = jnp.concatenate([green1[p, m, mine, :].astype(F32) for m in range(SIDE)], axis=1)
+    for p in range(2):
+        parts = [jnp.where(j == m, own1[p], green1[p, m, mine, :].astype(F32)) for m in range(SIDE)]
+        whole = jnp.concatenate(parts, axis=1)
         out[1, p] = exchanged(whole, chip)
     g_row0.near()
     g_image0.forward()
@@ -386,7 +406,9 @@
     for copy in tail:
         copy.wait_recv()
     for p in range(2):
-        whole = jnp.concatenate([final[m, p].astype(F32) for m in range(SIDE)], axis=1)
+        own0 = acc[p, mine, :]
+        parts = [jnp.where(j == m, own0, final[m, p].astype(F32)) for m in range(SIDE)]
+        whole = jnp.concatenate(parts, axis=1)
         out[0, p] = exchanged(whole, chip)
     for g in (g_row2, g_col1, g_row1, g_image1, g_green, g_col0, g_row0, g_image0):
         g.drain()
@@ -395,6 +417,7 @@
 
 
 def on_device(left_inverse, regions, region_mass, region_alpha, energy_grid, energy_index):
+    arrays = (left_inverse, regions, region_mass, region_alpha, energy_grid)
     count, _, rows, size = left_inverse.shape
     high, panel = SIDE * rows, SIDE * CORES * rows
     vmem = pl.BlockSpec(memory_space=pltpu.VMEM)
@@ -403,7 +426,7 @@
     return pl.pallas_call(
         kernel,
         out_shape=jax.ShapeDtypeStruct((count - 1, 2, rows, size), F32),
-        in_specs=[pl.BlockSpec(memory_space=pl.ANY), vmem, smem, smem, smem, smem],
+        in_specs=[pl.BlockSpec(memory_space=pl.ANY)] * 5 + [smem],
         out_specs=vmem,
         scratch_shapes=[
             pltpu.VMEM((2, SIDE, rows, size), BF),
@@ -424,11 +447,17 @@
             pltpu.SemaphoreType.DMA((copies,)),
             pltpu.SemaphoreType.DMA((copies,)),
             pltpu.SemaphoreType.DMA((8,)),
+            pltpu.VMEM((2, rows, panel), F32),
+            pltpu.VMEM(regions.shape, jnp.int32),
+            pltpu.SMEM(region_mass.shape, F32),
+            pltpu.SMEM(region_alpha.shape, F32),
+            pltpu.SMEM(energy_grid.shape, F32),
+            pltpu.SemaphoreType.DMA((4,)),
         ],
         compiler_params=pltpu.CompilerParams(
-            collective_id=0, has_side_effects=True, vmem_limit_bytes=60 * 1024 * 1024
+            collective_id=0, has_side_effects=True, vmem_limit_bytes=44 * 1024 * 1024
         ),
-    )(left_inverse, regions, region_mass, region_alpha, energy_grid, energy_index)
+    )(*(pltpu.with_memory_space_constraint(x, pltpu.HBM) for x in arrays), energy_index)
 
 
 def solution(mesh):

time: 73.2 us -> 70 us (0.956)
  Pallas kernels: 69.9 us -> 68.2 us
  local copies, waits for them, and re-layouts: 2.36 us -> 1.02 us
    pallas_call x1, Pallas kernels: 69.9 us -> 68.2 us  [on_device(): pl.pallas_call(kernel, out_shape=jax.ShapeDtypeStruct((count - 1, 2, rows...]
    unnamed x1, local copies, waits for them, and re-layouts: 2.36 us -> 1.02 us
where the time goes in v3:
time: 70 us; the launch traced here: 69.9 us
  Pallas kernels  68.2 us (97%)
  local copies, waits for them, and re-layouts  1.02 us (1%)
    pallas_call x1, Pallas kernels, on_device(): pl.pallas_call(kernel, out_shape=jax.ShapeDtypeStruct((count - 1, 2, rows...  68.2 us

profile of v3, /device:TPU:1, one launch (start us, length us, event | category | flops | bytes accessed | tf_op | source)
XLA Modules:
  0.0 69.9 jit_solution(11474678078637946399)
XLA Ops:
  0.7 68.2 %shard_map.64 = f32[2,2,48,1536]{3,2,1,0:T(8,128)S(1)} custom-call(bf16[3,2,48,1536]{3,2,1,0:T(8,128)(2,1)} %left.1, s32[3,1536]{1,0:T(4,128)} %regions_in.1, f32[3]{0:T(128)} %region_mass_in.1, f32[3]{0:T(128)} %region_alpha_in.1, f32[16]{0:T(128)} %energy_grid_in.1, s32[1]{0:T(128)S(6)} %copy.8.energy_index), custom_call_target="tpu_custom_call" | custom-call | tf_op jit(solution)/shard_map/pallas_call | solution.py:426
  68.8 1.0 %copy.9 = f32[2,2,48,1536]{3,2,1,0:T(8,128)} copy(f32[2,2,48,1536]{3,2,1,0:T(8,128)S(1)} %shard_map.64) | data formatting | bytes 2359296
